TPU v7x, 512 devices: a whole 4x4x16 slice. The times are simulated.
512 devices in a mesh: rep: 4 (over x), fsdp: 16 (over z), tp: 8 (over y, core).
Axes of the slice: x: 4, y: 4, z: 16, core: 2. Of those that a mesh axis runs over, the one named last changes fastest.
Arguments:
- tracker: bfloat16 [4, 4096, 14336], P('rep', 'fsdp', 'tp'), may hold values from -20 to 20
- grad_delta: bfloat16 [4, 4096, 14336], P('rep', 'fsdp', 'tp'), may hold values from -20 to 20
- momentum: bfloat16 [4, 4096, 14336], P('rep', 'fsdp', 'tp'), may hold values from -20 to 20
- q_basis: bfloat16 [4, 14336, 512], P('rep', 'tp', 'fsdp'), may hold values from -0.046875 to 0.046875
- mix_counts: int32 [4, 3], replicated, may hold values from 1 to 8
Outputs:
- new_tracker: bfloat16 [4, 4096, 14336], P('rep', 'fsdp', 'tp')
- new_momentum: bfloat16 [4, 4096, 14336], P('rep', 'fsdp', 'tp')
- left_basis: bfloat16 [4, 4096, 512], P('rep', 'fsdp')
- q_new: bfloat16 [4, 14336, 512], P('rep', 'tp', 'fsdp')
All inputs are finite; a program needn't handle non-finite values.
Results may differ from a plain program's by a relative error of at most 0.0061.
Values may be sent and summed in bfloat16 or wider, within the bound.
A program may use at most 64 MiB of HBM per device.

v0:
```python
import jax
import jax.numpy as jnp
from jax import lax
from jax.sharding import PartitionSpec as P

D = 4096
FF = 14336


def extended(block, sides, width):
    for axis, dim in sides:
        count = lax.axis_size(axis)
        forward = [(i, i + 1) for i in range(count - 1)]
        forward.append((count - 1, 0))
        backward = [(target, source) for source, target in forward]
        low = lax.ppermute(
            lax.slice_in_dim(block, block.shape[dim] - width, None, axis=dim), axis, forward
        )
        high = lax.ppermute(lax.slice_in_dim(block, 0, width, axis=dim), axis, backward)
        block = jnp.concatenate([low, block, high], axis=dim)
    return block


def orthonormal(pmat, gram):
    factor = jnp.linalg.cholesky(gram)
    solved = jax.scipy.linalg.solve_triangular(factor, pmat.T, lower=True).T
    return (solved * jnp.sqrt(jnp.float32(D))).astype(jnp.bfloat16)


def local(tracker, grad_delta, momentum, q_basis, mix_counts):
    agent = lax.axis_index("rep")
    counts = mix_counts.astype(jnp.float32)
    select = (jnp.arange(counts.shape[0]) == agent).astype(jnp.float32)
    mine = jnp.sum(select[:, None] * counts, axis=0)
    weights = mine / jnp.sum(mine)
    near = extended(tracker, (("rep", 0),), 1)
    mixed = (
        weights[0] * near[1].astype(jnp.float32)
        + weights[1] * near[0].astype(jnp.float32)
        + weights[2] * near[2].astype(jnp.float32)
    )
    tracked = mixed + grad_delta[0].astype(jnp.float32)
    new_tracker = tracked.astype(jnp.bfloat16)
    accum = momentum[0].astype(jnp.float32) + tracked
    accum_b = accum.astype(jnp.bfloat16)
    scale = 1.0 / jnp.sqrt(jnp.float32(D))
    basis_full = lax.all_gather(q_basis, "fsdp", axis=2, tiled=True)[0]
    partial_left = jnp.dot(accum_b, basis_full, preferred_element_type=jnp.float32)
    pmat = lax.psum(partial_left, "tp")
    gram_part = jnp.dot(pmat.T, pmat, precision=lax.Precision.HIGHEST)
    gram = lax.psum(gram_part, "fsdp")
    left_b = orthonormal(pmat, gram)
    block = left_b
    product = lax.dot_general(
        block, accum_b, (((0,), (0,)), ((), ())), preferred_element_type=jnp.float32
    )
    right_t = lax.psum_scatter(product * scale, "fsdp", scatter_dimension=0, tiled=True)
    squares = lax.psum(jnp.sum(right_t * right_t, axis=1), "tp")
    rms = jnp.sqrt(squares / FF) + 1e-06
    q_new = (right_t / rms[:, None]).T.astype(jnp.bfloat16)
    right_b = right_t.astype(jnp.bfloat16)
    block = left_b
    feed = jnp.dot(
        block,
        lax.all_gather(right_b, "fsdp", axis=0, tiled=True),
        preferred_element_type=jnp.float32,
    )
    new_momentum = (accum - 0.5 * scale * feed).astype(jnp.bfloat16)
    return (new_tracker[None], new_momentum[None], left_b[None], q_new[None])


def solution(mesh):
    in_specs = (
        P("rep", "fsdp", "tp"),
        P("rep", "fsdp", "tp"),
        P("rep", "fsdp", "tp"),
        P("rep", "tp", "fsdp"),
        P(),
    )
    out_specs = (
        P("rep", "fsdp", "tp"),
        P("rep", "fsdp", "tp"),
        P("rep", "fsdp", None),
        P("rep", "tp", "fsdp"),
    )
    return jax.shard_map(local, mesh=mesh, in_specs=in_specs, out_specs=out_specs, check_vma=False)
```

profile of v0, /device:TPU:2, one launch (start us, length us, event | category | flops | bytes accessed | tf_op | source)
XLA Modules:
  0.0 640.5 jit_solution(14598845073682928262)
XLA Ops:
  7.9 7.8 %collective-permute-start.1 = (bf16[1,256,1792]{2,1,0:T(8,128)(2,1)}, bf16[1,256,1792]{2,1,0:T(8,128)(2,1)S(1)}, u32[]{:S(2)}, u32[]{:S(2)}) collective-permute-start(bf16[1,256,1792]{2,1,0:T(8,128)(2,1)} %param.5), channel_id=1, source_target_pairs={{128,0},{256,128},{384,256},{0,384},{129,1},{257,129},{385,257},{1... | collective-permute-start | bytes 2752520 | tf_op jit(solution)/shard_map/ppermute | solution.py:19
  20.3 11.8 %collective-permute-done.1 = bf16[1,256,1792]{2,1,0:T(8,128)(2,1)S(1)} collective-permute-done((bf16[1,256,1792]{2,1,0:T(8,128)(2,1)}, bf16[1,256,1792]{2,1,0:T(8,128)(2,1)S(1)}, u32[]{:S(2)}, u32[]{:S(2)}) %collective-permute-start.1) | collective-permute-done | bytes 917536 | tf_op jit(solution)/shard_map/ppermute | solution.py:19
  32.1 3.2 collective-permute-done
  36.3 5.5 fusion.44
  41.8 45.7 %all-gather.3.cloned.1.call-done = bf16[1,1792,512]{1,2,0:T(8,128)(2,1)} async-done(((bf16[1,1792,32]{1,2,0:T(8,128)(2,1)}), bf16[1,1792,512]{1,2,0:T(8,128)(2,1)}) %all-gather.3.cloned.1.call-update) | async-done | bytes 1835024 | tf_op jit(solution)/shard_map/all_gather | solution.py:47
  87.5 3.0 fusion.3
  90.6 73.0 %all-reduce.4.cloned.1.call-done = f32[256,512]{1,0:T(8,128)} async-done(((f32[256,512]{1,0:T(8,128)}), f32[256,512]{1,0:T(8,128)}) %all-reduce.4.cloned.1.call-update) | async-done | bytes 524304 | tf_op jit(solution)/shard_map/psum | solution.py:49
  163.6 3.3 fusion.47
  167.1 138.0 %all-reduce.6.cloned.1.call-done = f32[512,512]{0,1:T(8,128)} async-done(((f32[512,512]{0,1:T(8,128)}), f32[512,512]{0,1:T(8,128)}) %all-reduce.6.cloned.1.call-update) | async-done | bytes 1048592 | tf_op jit(solution)/shard_map/psum | solution.py:51
  310.5 11.7 %cholesky.104 = f32[128,128]{1,0:T(8,128)S(1)} custom-call(f32[128,128]{1,0:T(8,128)S(1)} %cholesky.266), custom_call_target="Cholesky" | custom-call | tf_op jit(solution)/shard_map/jit(cholesky)/cholesky | solution.py:25
  323.4 9.8 %custom-call.31 = f32[1,128,128]{1,2,0:T(8,128)S(1)} custom-call(f32[1,128,128]{2,1,0:T(8,128)S(1)} %get-tuple-element.41), custom_call_target="InvertDiagBlocksLowerTriangular" | custom-call | tf_op jit(solution)/shard_map/jit(cholesky)/cholesky | solution.py:25
  336.5 11.7 %cholesky.217 = f32[128,128]{1,0:T(8,128)S(1)} custom-call(f32[128,128]{1,0:T(8,128)S(1)} %cholesky.270), custom_call_target="Cholesky" | custom-call | tf_op jit(solution)/shard_map/jit(cholesky)/cholesky | solution.py:25
  348.8 10.0 %custom-call.32 = f32[1,128,128]{1,2,0:T(8,128)S(1)} custom-call(f32[1,128,128]{2,1,0:T(8,128)S(1)} %get-tuple-element.38), custom_call_target="InvertDiagBlocksLowerTriangular" | custom-call | tf_op jit(solution)/shard_map/jit(cholesky)/cholesky | solution.py:25
  361.2 11.7 %cholesky.238 = f32[128,128]{1,0:T(8,128)S(1)} custom-call(f32[128,128]{1,0:T(8,128)S(1)} %cholesky.275), custom_call_target="Cholesky" | custom-call | tf_op jit(solution)/shard_map/jit(cholesky)/cholesky | solution.py:25
  373.6 9.8 %custom-call.33 = f32[1,128,128]{1,2,0:T(8,128)S(1)} custom-call(f32[1,128,128]{2,1,0:T(8,128)S(1)} %get-tuple-element.35), custom_call_target="InvertDiagBlocksLowerTriangular" | custom-call | tf_op jit(solution)/shard_map/jit(cholesky)/cholesky | solution.py:25
  385.6 11.7 %cholesky.255 = f32[128,128]{1,0:T(8,128)S(1)} custom-call(f32[128,128]{1,0:T(8,128)S(1)} %convolution_subtract_fusion.5), custom_call_target="Cholesky" | custom-call | tf_op jit(solution)/shard_map/jit(cholesky)/cholesky | solution.py:25
  405.1 14.5 %while.1 = (s32[]{:T(128)}, f32[512,512]{1,0:T(8,128)}, s32[4,2]{0,1:T(2,128)S(1)}, f32[4,128,128]{2,1,0:T(8,128)}, s32[]{:T(128)}) while((s32[]{:T(128)}, f32[512,512]{1,0:T(8,128)}, s32[4,2]{0,1:T(2,128)S(1)}, f32[4,128,128]{2,1,0:T(8,128)}, s32[]{:T(128)}) %tuple.37), condition=%wide.while_cond, body=%wide.while_body.sunk | while | flops 2 | bytes 132205 | solution.py:26
  405.8 3.0 bitcast_dynamic-update-slice_fusion.2
  413.1 3.0 bitcast_dynamic-update-slice_fusion.2
  419.6 40.8 %custom-call.34 = f32[4,128,128]{1,2,0:T(8,128)} custom-call(f32[4,128,128]{2,1,0:T(8,128)} %get-tuple-element.11), custom_call_target="InvertDiagBlocksLowerTriangular" | custom-call | tf_op jit(solution)/shard_map/jit(_solve_triangular)/triangular_solve | solution.py:26
  472.1 75.2 %reduce-scatter.2.cloned.1.call-done = f32[32,1792]{1,0:T(8,128)} async-done(((f32[512,1792]{1,0:T(8,128)}), f32[32,1792]{1,0:T(8,128)}) %reduce-scatter.2.cloned.1.call-update) | async-done | bytes 229392 | tf_op jit(solution)/shard_map/reduce_scatter | solution.py:57
  548.4 12.4 %psum.23 = f32[32]{0:T(128)S(1)} all-reduce(f32[32]{0:T(128)S(1)} %multiply_reduce_fusion), channel_id=1, replica_groups=mesh['rep'=4,'fsdp'=16,'tp'=8] {'tp'}, use_global_device_ids=true, to_apply=%region_14.15 | all-reduce | flops 32 | bytes 256 | tf_op jit(solution)/shard_map/psum | solution.py:58
  563.5 67.4 %all-gather.5.cloned.1.call-done = bf16[512,1792]{1,0:T(8,128)(2,1)} async-done(((bf16[32,1792]{1,0:T(8,128)(2,1)}), bf16[512,1792]{1,0:T(8,128)(2,1)}) %all-gather.5.cloned.1.call-update) | async-done | bytes 1835024 | tf_op jit(solution)/shard_map/all_gather | solution.py:65
  630.9 3.1 fusion.2
  (75 shorter events, 51.4 us)
Async XLA Ops:
  7.2 80.3 %all-gather.3.cloned.1.call-start = ((), (), s32[]{:S(2)}) async-start(), calls=%async_computation.1 | async-start | bytes 1949696 | tf_op jit(solution)/shard_map/all_gather | solution.py:47
  7.9 155.7 %all-reduce.4.cloned.1.call-start = ((), (), s32[]{:S(2)}) async-start(), calls=%async_computation.2 | async-start | bytes 1048576 | tf_op jit(solution)/shard_map/psum | solution.py:49
  7.9 24.2 %collective-permute-start.1 = (bf16[1,256,1792]{2,1,0:T(8,128)(2,1)}, bf16[1,256,1792]{2,1,0:T(8,128)(2,1)S(1)}, u32[]{:S(2)}, u32[]{:S(2)}) collective-permute-start(bf16[1,256,1792]{2,1,0:T(8,128)(2,1)} %param.5), channel_id=1, source_target_pairs={{128,0},{256,128},{384,256},{0,384},{129,1},{257,129},{385,257},{1... | collective-permute-start | bytes 2752520 | tf_op jit(solution)/shard_map/ppermute | solution.py:19
  15.8 19.6 %collective-permute-start = (bf16[1,256,1792]{2,1,0:T(8,128)(2,1)}, bf16[1,256,1792]{2,1,0:T(8,128)(2,1)S(1)}, u32[]{:S(2)}, u32[]{:S(2)}) collective-permute-start(bf16[1,256,1792]{2,1,0:T(8,128)(2,1)} %param.5), channel_id=1, source_target_pairs={{0,128},{128,256},{256,384},{384,0},{1,129},{129,257},{257,385},{3... | collective-permute-start | bytes 2752520 | tf_op jit(solution)/shard_map/ppermute | solution.py:16
  32.1 3.2 copy-start.5
  35.3 0.9 copy-start.6
  36.3 51.2 %copy-start = (bf16[1,256,1792]{2,1,0:T(8,128)(2,1)S(1)}, bf16[1,256,1792]{2,1,0:T(8,128)(2,1)}, u32[]{:S(2)}) copy-start(bf16[1,256,1792]{2,1,0:T(8,128)(2,1)} %param.7) | copy-start | bytes 2752516
  90.5 214.6 %all-reduce.6.cloned.1.call-start = ((), (), s32[]{:S(2)}) async-start(), calls=%async_computation.3 | async-start | bytes 2097152 | tf_op jit(solution)/shard_map/psum | solution.py:51
  166.9 380.4 %reduce-scatter.2.cloned.1.call-start = ((), (), s32[]{:S(2)}) async-start(), calls=%async_computation.4 | async-start | bytes 3899392 | tf_op jit(solution)/shard_map/reduce_scatter | solution.py:57
  309.5 1.0 copy-start.4
  373.6 86.8 %copy-start.1 = (f32[256,512]{1,0:T(8,128)S(1)}, f32[256,512]{1,0:T(8,128)}, u32[]{:S(2)}) copy-start(f32[256,512]{1,0:T(8,128)} %all-reduce.4.cloned.1.call-done) | copy-start | bytes 1572868
  466.6 3.0 copy-start.2
  472.0 90.6 %copy-start.3 = (f32[128,256]{1,0:T(8,128)S(1)}, f32[128,256]{1,0:T(8,128)}, u32[]{:S(2)}) copy-start(f32[128,256]{1,0:T(8,128)} %copy-done.2) | copy-start | bytes 393220
  472.1 158.8 %all-gather.5.cloned.1.call-start = ((), (), s32[]{:S(2)}) async-start(), calls=%async_computation.5 | async-start | bytes 1949696 | tf_op jit(solution)/shard_map/all_gather | solution.py:65
Sparse Core Ops, SparseCore 0:
  10.1 77.3 all-gather.2
  90.6 72.8 all-reduce.3
  167.0 138.0 all-reduce.5
  472.2 75.0 reduce-scatter.1
  562.7 68.1 all-gather.4
where the time goes:
time: 642 us; the launch traced here: 641 us
  waiting for transfers between devices  415 us (65%)
  other arithmetic  136 us (21%)
  matrix products  28.8 us (4%)
  local copies, waits for them, and re-layouts  21.6 us (3%)
  between operations  16.5 us (3%)
  blocking collectives  12.4 us (2%)
  starting transfers between devices  10.1 us (2%)
    psum x1, waiting for transfers between devices, local(): gram = lax.psum(gram_part, 'fsdp')  138 us
    another operation x14, other arithmetic, orthonormal(): factor = jnp.linalg.cholesky(gram)  80.4 us
    reduce_scatter x1, waiting for transfers between devices, local(): lax.psum_scatter(product * scale, 'fsdp', scatter_dimension=0, tiled=True)  75.2 us
    psum x1, waiting for transfers between devices, local(): pmat = lax.psum(partial_left, 'tp')  73 us
    all_gather x1, waiting for transfers between devices, local(): lax.all_gather(right_b, 'fsdp', axis=0, tiled=True)  67.4 us
    all_gather x1, waiting for transfers between devices, local(): basis_full = lax.all_gather(q_basis, 'fsdp', axis=2, tiled=True)[0]  45.7 us
    another operation x3, other arithmetic, orthonormal(): solved = jax.scipy.linalg.solve_triangular(factor, pmat.T, lower=True).T  43.4 us
    another operation x12, local copies, waits for them, and re-layouts  14.5 us
  transfers between devices with their start and end apart: 7, of which 7 were waited for; matrix products, arithmetic and copies ran while one was open for 1% of the time, Pallas kernels for 0%

commit v1 on v0

--- a/solution.py
+++ b/solution.py
@@ -48,7 +48,9 @@
     partial_left = jnp.dot(accum_b, basis_full, preferred_element_type=jnp.float32)
     pmat = lax.psum(partial_left, "tp")
     gram_part = jnp.dot(pmat.T, pmat, precision=lax.Precision.HIGHEST)
-    gram = lax.psum(gram_part, "fsdp")
+    gram = gram_part
+    for hop in (1, 2, 4, 8):
+        gram = gram + lax.ppermute(gram, "fsdp", [(dev, dev ^ hop) for dev in range(16)])
     left_b = orthonormal(pmat, gram)
     block = left_b
     product = lax.dot_general(

time: 642 us -> 771 us (1.20)
  waiting for transfers between devices: 415 us -> 522 us
  starting transfers between devices: 10.1 us -> 37.1 us
    ppermute x0 -> x4, waiting for transfers between devices: none -> 220 us  [local(): lax.ppermute(gram, 'fsdp', [(dev, dev ^ hop) for dev in range(16)])]
    psum x1 -> x0, waiting for transfers between devices: 138 us -> none  [local(): gram = lax.psum(gram_part, 'fsdp')]
    ppermute x0 -> x4, starting transfers between devices: none -> 27.2 us  [local(): lax.ppermute(gram, 'fsdp', [(dev, dev ^ hop) for dev in range(16)])]
    reduce_scatter x1, waiting for transfers between devices: 75.2 us -> 99.6 us  [local(): lax.psum_scatter(product * scale, 'fsdp', scatter_dimension=0, tiled=True)]
  transfers between devices with their start and end apart: 7 -> 10, of which waited for: 7 -> 10; matrix products, arithmetic and copies ran while one was open for 1% -> 1% of each run, Pallas kernels for 0% -> 0%
where the time goes in v1:
time: 771 us; the launch traced here: 770 us
  waiting for transfers between devices  522 us (68%)
  other arithmetic  137 us (18%)
  starting transfers between devices  37.1 us (5%)
  matrix products  26.2 us (3%)
  local copies, waits for them, and re-layouts  18.9 us (2%)
  between operations  16.6 us (2%)
  blocking collectives  12.4 us (2%)
    ppermute x4, waiting for transfers between devices, local(): lax.ppermute(gram, 'fsdp', [(dev, dev ^ hop) for dev in range(16)])  220 us
    reduce_scatter x1, waiting for transfers between devices, local(): lax.psum_scatter(product * scale, 'fsdp', scatter_dimension=0, tiled=True)  99.6 us
    another operation x14, other arithmetic, orthonormal(): factor = jnp.linalg.cholesky(gram)  81 us
    psum x1, waiting for transfers between devices, local(): pmat = lax.psum(partial_left, 'tp')  73 us
    all_gather x1, waiting for transfers between devices, local(): lax.all_gather(right_b, 'fsdp', axis=0, tiled=True)  67.5 us
    all_gather x1, waiting for transfers between devices, local(): basis_full = lax.all_gather(q_basis, 'fsdp', axis=2, tiled=True)[0]  45.7 us
    another operation x3, other arithmetic, orthonormal(): solved = jax.scipy.linalg.solve_triangular(factor, pmat.T, lower=True).T  42 us
    ppermute x4, starting transfers between devices, local(): lax.ppermute(gram, 'fsdp', [(dev, dev ^ hop) for dev in range(16)])  27.2 us
  transfers between devices with their start and end apart: 10, of which 10 were waited for; matrix products, arithmetic and copies ran while one was open for 1% of the time, Pallas kernels for 0%

profile of v1, /device:TPU:2, one launch (start us, length us, event | category | flops | bytes accessed | tf_op | source)
XLA Modules:
  0.0 770.2 jit_solution(9823541892567727847)
XLA Ops:
  7.9 7.8 %collective-permute-start.1 = (bf16[1,256,1792]{2,1,0:T(8,128)(2,1)}, bf16[1,256,1792]{2,1,0:T(8,128)(2,1)S(1)}, u32[]{:S(2)}, u32[]{:S(2)}) collective-permute-start(bf16[1,256,1792]{2,1,0:T(8,128)(2,1)} %param.5), channel_id=1, source_target_pairs={{128,0},{256,128},{384,256},{0,384},{129,1},{257,129},{385,257},{1... | collective-permute-start | bytes 2752520 | tf_op jit(solution)/shard_map/ppermute | solution.py:19
  20.3 11.8 %collective-permute-done.1 = bf16[1,256,1792]{2,1,0:T(8,128)(2,1)S(1)} collective-permute-done((bf16[1,256,1792]{2,1,0:T(8,128)(2,1)}, bf16[1,256,1792]{2,1,0:T(8,128)(2,1)S(1)}, u32[]{:S(2)}, u32[]{:S(2)}) %collective-permute-start.1) | collective-permute-done | bytes 917536 | tf_op jit(solution)/shard_map/ppermute | solution.py:19
  36.3 5.5 fusion.49
  41.8 45.7 %all-gather.3.cloned.1.call-done = bf16[1,1792,512]{1,2,0:T(8,128)(2,1)} async-done(((bf16[1,1792,32]{1,2,0:T(8,128)(2,1)}), bf16[1,1792,512]{1,2,0:T(8,128)(2,1)}) %all-gather.3.cloned.1.call-update) | async-done | bytes 1835024 | tf_op jit(solution)/shard_map/all_gather | solution.py:47
  90.6 73.0 %all-reduce.3.cloned.1.call-done = f32[256,512]{1,0:T(8,128)} async-done(((f32[256,512]{1,0:T(8,128)}), f32[256,512]{1,0:T(8,128)}) %all-reduce.3.cloned.1.call-update) | async-done | bytes 524304 | tf_op jit(solution)/shard_map/psum | solution.py:49
  169.3 21.3 %collective-permute-done.2 = f32[512,512]{0,1:T(8,128)S(1)} collective-permute-done((f32[512,512]{0,1:T(8,128)S(1)}, f32[512,512]{0,1:T(8,128)S(1)}, u32[]{:S(2)}, u32[]{:S(2)}) %collective-permute-start.2) | collective-permute-done | bytes 1048608 | tf_op jit(solution)/shard_map/ppermute | solution.py:53
  190.8 4.5 collective-permute-start.3
  195.3 42.7 %collective-permute-done.3 = f32[512,512]{0,1:T(8,128)S(1)} collective-permute-done((f32[512,512]{0,1:T(8,128)S(1)}, f32[512,512]{0,1:T(8,128)S(1)}, u32[]{:S(2)}, u32[]{:S(2)}) %collective-permute-start.3) | collective-permute-done | bytes 1048608 | tf_op jit(solution)/shard_map/ppermute | solution.py:53
  238.2 7.6 collective-permute-start.4
  245.9 111.5 %collective-permute-done.4 = f32[512,512]{0,1:T(8,128)S(1)} collective-permute-done((f32[512,512]{0,1:T(8,128)S(1)}, f32[512,512]{0,1:T(8,128)S(1)}, u32[]{:S(2)}, u32[]{:S(2)}) %collective-permute-start.4) | collective-permute-done | bytes 1048608 | tf_op jit(solution)/shard_map/ppermute | solution.py:53
  357.6 11.6 %collective-permute-start.5 = (f32[512,512]{0,1:T(8,128)S(1)}, f32[512,512]{0,1:T(8,128)}, u32[]{:S(2)}, u32[]{:S(2)}) collective-permute-start(f32[512,512]{0,1:T(8,128)S(1)} %add.101), channel_id=1, source_target_pairs={{0,64},{8,72},{16,80},{24,88},{32,96},{40,104},{48,112},{56,120},{... | collective-permute-start | bytes 3145736 | tf_op jit(solution)/shard_map/ppermute | solution.py:53
  369.3 44.7 %collective-permute-done.5 = f32[512,512]{0,1:T(8,128)} collective-permute-done((f32[512,512]{0,1:T(8,128)S(1)}, f32[512,512]{0,1:T(8,128)}, u32[]{:S(2)}, u32[]{:S(2)}) %collective-permute-start.5) | collective-permute-done | bytes 1048608 | tf_op jit(solution)/shard_map/ppermute | solution.py:53
  419.5 11.7 %cholesky.104 = f32[128,128]{1,0:T(8,128)S(1)} custom-call(f32[128,128]{1,0:T(8,128)S(1)} %cholesky.266), custom_call_target="Cholesky" | custom-call | tf_op jit(solution)/shard_map/jit(cholesky)/cholesky | solution.py:25
  431.4 9.8 %custom-call.31 = f32[1,128,128]{1,2,0:T(8,128)S(1)} custom-call(f32[1,128,128]{2,1,0:T(8,128)S(1)} %get-tuple-element.41), custom_call_target="InvertDiagBlocksLowerTriangular" | custom-call | tf_op jit(solution)/shard_map/jit(cholesky)/cholesky | solution.py:25
  443.7 11.7 %cholesky.217 = f32[128,128]{1,0:T(8,128)S(1)} custom-call(f32[128,128]{1,0:T(8,128)S(1)} %cholesky.270), custom_call_target="Cholesky" | custom-call | tf_op jit(solution)/shard_map/jit(cholesky)/cholesky | solution.py:25
  455.4 10.0 %custom-call.32 = f32[1,128,128]{1,2,0:T(8,128)S(1)} custom-call(f32[1,128,128]{2,1,0:T(8,128)S(1)} %get-tuple-element.38), custom_call_target="InvertDiagBlocksLowerTriangular" | custom-call | tf_op jit(solution)/shard_map/jit(cholesky)/cholesky | solution.py:25
  467.0 11.7 %cholesky.238 = f32[128,128]{1,0:T(8,128)S(1)} custom-call(f32[128,128]{1,0:T(8,128)S(1)} %cholesky.275), custom_call_target="Cholesky" | custom-call | tf_op jit(solution)/shard_map/jit(cholesky)/cholesky | solution.py:25
  479.4 11.3 %custom-call.33 = f32[1,128,128]{1,2,0:T(8,128)} custom-call(f32[1,128,128]{2,1,0:T(8,128)} %get-tuple-element.35), custom_call_target="InvertDiagBlocksLowerTriangular" | custom-call | tf_op jit(solution)/shard_map/jit(cholesky)/cholesky | solution.py:25
  493.0 11.7 %cholesky.255 = f32[128,128]{1,0:T(8,128)S(1)} custom-call(f32[128,128]{1,0:T(8,128)S(1)} %slice_subtract_fusion.2), custom_call_target="Cholesky" | custom-call | tf_op jit(solution)/shard_map/jit(cholesky)/cholesky | solution.py:25
  510.6 14.0 %while.1 = (s32[]{:T(128)}, f32[512,512]{1,0:T(8,128)}, s32[4,2]{0,1:T(2,128)S(1)}, f32[4,128,128]{2,1,0:T(8,128)}, s32[]{:T(128)}) while((s32[]{:T(128)}, f32[512,512]{1,0:T(8,128)}, s32[4,2]{0,1:T(2,128)S(1)}, f32[4,128,128]{2,1,0:T(8,128)}, s32[]{:T(128)}) %tuple.37), condition=%wide.while_cond, body=%wide.while_body.sunk | while | flops 2 | bytes 132205 | solution.py:26
  524.7 40.8 %custom-call.34 = f32[4,128,128]{1,2,0:T(8,128)} custom-call(f32[4,128,128]{2,1,0:T(8,128)} %get-tuple-element.11), custom_call_target="InvertDiagBlocksLowerTriangular" | custom-call | tf_op jit(solution)/shard_map/jit(_solve_triangular)/triangular_solve | solution.py:26
  577.2 99.6 %reduce-scatter.2.cloned.1.call-done = f32[32,1792]{1,0:T(8,128)} async-done(((f32[512,1792]{1,0:T(8,128)}), f32[32,1792]{1,0:T(8,128)}) %reduce-scatter.2.cloned.1.call-update) | async-done | bytes 229392 | tf_op jit(solution)/shard_map/reduce_scatter | solution.py:59
  677.9 12.4 %psum.15 = f32[32]{0:T(128)S(1)} all-reduce(f32[32]{0:T(128)S(1)} %multiply_reduce_fusion), channel_id=1, replica_groups=mesh['rep'=4,'fsdp'=16,'tp'=8] {'tp'}, use_global_device_ids=true, to_apply=%region_13.14 | all-reduce | flops 32 | bytes 256 | tf_op jit(solution)/shard_map/psum | solution.py:60
  693.1 67.5 %all-gather.5.cloned.1.call-done = bf16[512,1792]{1,0:T(8,128)(2,1)} async-done(((bf16[32,1792]{1,0:T(8,128)(2,1)}), bf16[512,1792]{1,0:T(8,128)(2,1)}) %all-gather.5.cloned.1.call-update) | async-done | bytes 1835024 | tf_op jit(solution)/shard_map/all_gather | solution.py:67
  (88 shorter events, 67.4 us)
Async XLA Ops:
  7.2 80.3 %all-gather.3.cloned.1.call-start = ((), (), s32[]{:S(2)}) async-start(), calls=%async_computation.1 | async-start | bytes 1949696 | tf_op jit(solution)/shard_map/all_gather | solution.py:47
  7.9 155.7 %all-reduce.3.cloned.1.call-start = ((), (), s32[]{:S(2)}) async-start(), calls=%async_computation.2 | async-start | bytes 1048576 | tf_op jit(solution)/shard_map/psum | solution.py:49
  7.9 24.2 %collective-permute-start.1 = (bf16[1,256,1792]{2,1,0:T(8,128)(2,1)}, bf16[1,256,1792]{2,1,0:T(8,128)(2,1)S(1)}, u32[]{:S(2)}, u32[]{:S(2)}) collective-permute-start(bf16[1,256,1792]{2,1,0:T(8,128)(2,1)} %param.5), channel_id=1, source_target_pairs={{128,0},{256,128},{384,256},{0,384},{129,1},{257,129},{385,257},{1... | collective-permute-start | bytes 2752520 | tf_op jit(solution)/shard_map/ppermute | solution.py:19
  15.8 19.6 %collective-permute-start = (bf16[1,256,1792]{2,1,0:T(8,128)(2,1)}, bf16[1,256,1792]{2,1,0:T(8,128)(2,1)S(1)}, u32[]{:S(2)}, u32[]{:S(2)}) collective-permute-start(bf16[1,256,1792]{2,1,0:T(8,128)(2,1)} %param.5), channel_id=1, source_target_pairs={{0,128},{128,256},{256,384},{384,0},{1,129},{129,257},{257,385},{3... | collective-permute-start | bytes 2752520 | tf_op jit(solution)/shard_map/ppermute | solution.py:16
  32.1 3.2 copy-start.7
  35.3 0.9 copy-start.8
  36.3 51.2 %copy-start = (bf16[1,256,1792]{2,1,0:T(8,128)(2,1)S(1)}, bf16[1,256,1792]{2,1,0:T(8,128)(2,1)}, u32[]{:S(2)}) copy-start(bf16[1,256,1792]{2,1,0:T(8,128)(2,1)} %param.7) | copy-start | bytes 2752516
  90.5 586.4 %reduce-scatter.2.cloned.1.call-start = ((), (), s32[]{:S(2)}) async-start(), calls=%async_computation.3 | async-start | bytes 3899392 | tf_op jit(solution)/shard_map/reduce_scatter | solution.py:59
  165.8 24.8 %collective-permute-start.2 = (f32[512,512]{0,1:T(8,128)S(1)}, f32[512,512]{0,1:T(8,128)S(1)}, u32[]{:S(2)}, u32[]{:S(2)}) collective-permute-start(f32[512,512]{0,1:T(8,128)S(1)} %fusion.52), channel_id=1, source_target_pairs={{0,8},{8,0},{16,24},{24,16},{32,40},{40,32},{48,56},{56,48},{64,72... | collective-permute-start | bytes 3145736 | tf_op jit(solution)/shard_map/ppermute | solution.py:53
  190.8 47.2 %collective-permute-start.3 = (f32[512,512]{0,1:T(8,128)S(1)}, f32[512,512]{0,1:T(8,128)S(1)}, u32[]{:S(2)}, u32[]{:S(2)}) collective-permute-start(f32[512,512]{0,1:T(8,128)S(1)} %add.99), channel_id=1, source_target_pairs={{0,16},{8,24},{16,0},{24,8},{32,48},{40,56},{48,32},{56,40},{64,80... | collective-permute-start | bytes 3145736 | tf_op jit(solution)/shard_map/ppermute | solution.py:53
  238.2 119.2 %collective-permute-start.4 = (f32[512,512]{0,1:T(8,128)S(1)}, f32[512,512]{0,1:T(8,128)S(1)}, u32[]{:S(2)}, u32[]{:S(2)}) collective-permute-start(f32[512,512]{0,1:T(8,128)S(1)} %add.100), channel_id=1, source_target_pairs={{0,32},{8,40},{16,48},{24,56},{32,0},{40,8},{48,16},{56,24},{64,96... | collective-permute-start | bytes 3145736 | tf_op jit(solution)/shard_map/ppermute | solution.py:53
  357.6 11.6 %copy-start.3 = (f32[512,512]{0,1:T(8,128)}, f32[512,512]{0,1:T(8,128)S(1)}, u32[]{:S(2)}) copy-start(f32[512,512]{0,1:T(8,128)S(1)} %add.101) | copy-start | bytes 3145732
  357.6 56.3 %collective-permute-start.5 = (f32[512,512]{0,1:T(8,128)S(1)}, f32[512,512]{0,1:T(8,128)}, u32[]{:S(2)}, u32[]{:S(2)}) collective-permute-start(f32[512,512]{0,1:T(8,128)S(1)} %add.101), channel_id=1, source_target_pairs={{0,64},{8,72},{16,80},{24,88},{32,96},{40,104},{48,112},{56,120},{... | collective-permute-start | bytes 3145736 | tf_op jit(solution)/shard_map/ppermute | solution.py:53
  418.5 1.0 copy-start.6
  479.4 86.1 %copy-start.2 = (f32[256,512]{1,0:T(8,128)S(1)}, f32[256,512]{1,0:T(8,128)}, u32[]{:S(2)}) copy-start(f32[256,512]{1,0:T(8,128)} %all-reduce.3.cloned.1.call-done) | copy-start | bytes 1572868
  524.7 50.0 %copy-start.1 = (bf16[1,256,1792]{2,1,0:T(8,128)(2,1)S(1)}, bf16[1,256,1792]{2,1,0:T(8,128)(2,1)}, u32[]{:S(2)}) copy-start(bf16[1,256,1792]{2,1,0:T(8,128)(2,1)} %param.7) | copy-start | bytes 2752516
  571.7 3.0 copy-start.4
  577.2 115.0 %copy-start.5 = (f32[128,256]{1,0:T(8,128)S(1)}, f32[128,256]{1,0:T(8,128)}, u32[]{:S(2)}) copy-start(f32[128,256]{1,0:T(8,128)} %copy-done.4) | copy-start | bytes 393220
  577.2 183.4 %all-gather.5.cloned.1.call-start = ((), (), s32[]{:S(2)}) async-start(), calls=%async_computation.4 | async-start | bytes 1949696 | tf_op jit(solution)/shard_map/all_gather | solution.py:67
Sparse Core Ops, SparseCore 0:
  10.1 77.3 all-gather.2
  90.6 72.8 all-reduce.2
  577.3 99.5 reduce-scatter.1
  692.3 68.2 all-gather.4
